TPU v7x, 256 devices: a whole 4x4x8 slice. The times are simulated.
256 devices in a mesh: feat: 64 (over x, y_hi, z), tgt: 4 (over y_lo, core).
Axes of the slice: x: 4, y: 4 (y_hi: 2, y_lo: 2; y = y_hi * 2 + y_lo), z: 8, core: 2. Of those that a mesh axis runs over, the one named last changes fastest.
Arguments:
- sources: bfloat16 [4, 128, 2304], P('tgt'), may hold values from -6 to 6
- targets: bfloat16 [4, 128, 2304], P('tgt', 'feat'), may hold values from -6 to 6
- enc_weight: bfloat16 [4, 2304, 16384], P('tgt', None, 'feat'), may hold values from -0.125 to 0.125
- enc_bias: float32 [4, 16384], P('tgt', 'feat'), may hold values from -5 to 5
- dec_weight: bfloat16 [4, 4, 16384, 2304], P('tgt', None, 'feat'), may hold values from -0.046875 to 0.046875
- pair_mask: int32 [4, 4], replicated, may hold values from 0 to 1, as said below
Outputs:
- error: bfloat16 [4, 128, 2304], P('tgt', 'feat')
- latent_grad: bfloat16 [4, 128, 16384], P('tgt', None, 'feat')
Inputs may be any that keep to these rules, and one draw needn't show every extreme that they name: pair_mask[t, s] is 0 wherever s > t and 1 wherever s == t.
All inputs are finite; a program needn't handle non-finite values.
Results may differ from a plain program's by a relative error of at most 0.0055.
Values may be sent and summed in bfloat16 or wider, within the bound.
No kernel may reach another device: no remote copies, remote signals or barrier semaphores. Data moves between devices by JAX's collectives and lax.ppermute only.
A program may use at most 64 MiB of HBM per device.

v0:
```python
import jax
import jax.numpy as jnp
from jax import lax
from jax.sharding import PartitionSpec as P


def per_device(sources, targets, enc_weight, enc_bias, dec_weight, pair_mask):
    layer_count = dec_weight.shape[1]
    width = sources.shape[2]
    rows_local = targets.shape[1]
    pre = jnp.dot(sources[0], enc_weight[0], preferred_element_type=jnp.float32) + enc_bias[0]
    latent = jnp.maximum(pre, 0.0).astype(jnp.bfloat16)
    latent_all = lax.all_gather(latent[None], "tgt", axis=0, tiled=True)
    owner = lax.axis_index("tgt")
    mask_row = lax.dynamic_index_in_dim(pair_mask, owner, 0, keepdims=False)
    total = jnp.zeros((rows_local * lax.axis_size("feat"), width), jnp.float32)
    for recon_source in range(layer_count):
        rows = latent_all[recon_source]
        recon_weight = mask_row[recon_source].astype(jnp.float32)
        total = total + recon_weight * jnp.dot(
            rows, dec_weight[0, recon_source], preferred_element_type=jnp.float32
        )
    share = lax.psum_scatter(total, "feat", scatter_dimension=0, tiled=True)
    err_local = (share - targets[0].astype(jnp.float32)).astype(jnp.bfloat16)
    err_full = lax.all_gather(err_local, "feat", axis=0, tiled=True)
    terms = []
    for source in range(layer_count):
        weight = mask_row[source].astype(jnp.float32)
        term = weight * lax.dot_general(
            err_full,
            dec_weight[0, source],
            (((1,), (1,)), ((), ())),
            preferred_element_type=jnp.float32,
        )
        terms.append(term)
    stacked = jnp.stack(terms)
    grads = lax.psum_scatter(stacked, "tgt", scatter_dimension=0, tiled=True)
    return (err_local[None], grads.astype(jnp.bfloat16))


def solution(mesh):
    in_specs = (
        P("tgt", None, None),
        P("tgt", "feat", None),
        P("tgt", None, "feat"),
        P("tgt", "feat"),
        P("tgt", None, "feat", None),
        P(),
    )
    out_specs = (P("tgt", "feat", None), P("tgt", None, "feat"))
    return jax.shard_map(
        per_device, mesh=mesh, in_specs=in_specs, out_specs=out_specs, check_vma=False
    )
```

profile of v0, /device:TPU:1, one launch (start us, length us, event | category | flops | bytes accessed | tf_op | source)
XLA Modules:
  0.0 911.5 jit_solution(5537049860476209958)
XLA Ops:
  7.2 0.0 copy-start
  7.2 0.0 all-reduce.3.cloned.1.call-start
  7.2 0.8 constant_dynamic-slice_fusion
  8.0 0.7 fusion.65
  9.2 0.0 copy-done
  9.2 1.4 fusion.47
  10.7 8.8 all-gather
  21.5 0.0 copy-start.1
  21.5 1.8 convolution_multiply_fusion.3
  23.2 1.6 fusion.2
  24.8 0.0 copy-done.1
  24.9 0.3 fusion.1
  25.2 1.4 fusion
  26.6 0.0 copy-start.4
  26.6 0.0 copy-start.3
  26.6 0.0 all-reduce.3.cloned.1.call-update
  26.6 0.0 reduce-scatter.2.cloned.1.call-start
  26.6 0.6 copy-done.4
  27.2 0.6 dynamic-slice
  28.5 633.8 %all-reduce.3.cloned.1.call-done = f32[128,2304]{1,0:T(8,128)} async-done(((f32[128,2304]{1,0:T(8,128)}), f32[128,2304]{1,0:T(8,128)}) %all-reduce.3.cloned.1.call-update) | async-done | bytes 1179664
  662.3 0.0 copy-done.3
  662.3 0.9 fusion.64
  663.2 0.0 copy-start.2
  663.2 155.4 %all-gather.1 = bf16[64,2,2304]{2,1,0:T(2,128)(2,1)S(1)} all-gather(bf16[1,2,2304]{2,1,0:T(2,128)(2,1)S(1)} %fusion.64), channel_id=1, replica_groups=mesh['feat'=64,'tgt'=4] {'feat'}, dimensions={0}, use_global_device_ids=true | all-gather | bytes 599040 | tf_op jit(solution)/shard_map/all_gather | solution.py:25
  818.6 0.2 reshape.29
  818.8 1.8 fusion.26
  820.6 0.0 copy-done.2
  820.6 1.8 fusion.32
  822.4 1.8 fusion.38
  824.3 1.8 fusion.44
  826.1 0.8 pad_maximum_fusion
  826.9 0.0 reduce-scatter.2.cloned.1.call-update
  827.0 76.1 %reduce-scatter.2.cloned.1.call-done = f32[1,128,256]{2,1,0:T(8,128)} async-done(((f32[4,128,256]{2,1,0:T(8,128)}), f32[1,128,256]{2,1,0:T(8,128)}) %reduce-scatter.2.cloned.1.call-update) | async-done | bytes 131088 | tf_op jit(solution)/shard_map/reduce_scatter | solution.py:37
  903.1 1.5 convert_element_type.55
Async XLA Ops:
  7.2 2.1 copy-start
  7.2 655.1 %all-reduce.3.cloned.1.call-start = ((), (), s32[]{:S(2)}) async-start(), calls=%async_computation.2 | async-start | bytes 2359296
  21.5 3.4 copy-start.1
  26.6 0.7 copy-start.4
  26.6 635.7 %copy-start.3 = (bf16[1,2,2304]{2,1,0:T(2,128)(2,1)S(1)}, bf16[1,2,2304]{2,1,0:T(2,128)(2,1)}, u32[]{:S(2)}) copy-start(bf16[1,2,2304]{2,1,0:T(2,128)(2,1)} %param.7) | copy-start | bytes 27652
  26.6 876.5 %reduce-scatter.2.cloned.1.call-start = ((), (), s32[]{:S(2)}) async-start(), calls=%async_computation.1 | async-start | bytes 655360 | tf_op jit(solution)/shard_map/reduce_scatter | solution.py:37
  663.2 157.5 %copy-start.2 = (bf16[1,2,2304]{2,1,0:T(2,128)(2,1)}, bf16[1,2,2304]{2,1,0:T(2,128)(2,1)S(1)}, u32[]{:S(2)}) copy-start(bf16[1,2,2304]{2,1,0:T(2,128)(2,1)S(1)} %fusion.64) | copy-start | bytes 27652
Sparse Core Ops, SparseCore 0:
  26.7 635.5 all-reduce.2
  827.1 75.9 reduce-scatter.1
where the time goes:
time: 912 us; the launch traced here: 911 us
  waiting for transfers between devices  710 us (78%)
  blocking collectives  164 us (18%)
  between operations  17.4 us (2%)
  matrix products  13.7 us (2%)
    unnamed x3, waiting for transfers between devices  634 us
    all_gather x1, blocking collectives, per_device(): err_full = lax.all_gather(err_local, 'feat', axis=0, tiled=True)  155 us
    reduce_scatter x1, waiting for transfers between devices, per_device(): grads = lax.psum_scatter(stacked, 'tgt', scatter_dimension=0, tiled=True)  76.1 us
  transfers between devices with their start and end apart: 2, of which 2 were waited for; matrix products, arithmetic and copies ran while one was open for 0% of the time, Pallas kernels for 0%

commit v1 on v0

--- a/solution.py
+++ b/solution.py
@@ -22,7 +22,9 @@
         )
     share = lax.psum_scatter(total, "feat", scatter_dimension=0, tiled=True)
     err_local = (share - targets[0].astype(jnp.float32)).astype(jnp.bfloat16)
-    err_full = lax.all_gather(err_local, "feat", axis=0, tiled=True)
+    err_full = jnp.concatenate(
+        lax.all_to_all(jnp.stack([err_local] * lax.axis_size("feat")), "feat", 0, 0), axis=0
+    )
     terms = []
     for source in range(layer_count):
         weight = mask_row[source].astype(jnp.float32)

time: 912 us -> 756 us (0.83)
  blocking collectives: 164 us -> 31.1 us
  waiting for transfers between devices: 710 us -> 687 us
    all_gather x1 -> x0, blocking collectives: 155 us -> none  [per_device(): err_full = lax.all_gather(err_local, 'feat', axis=0, tiled=True)]
    reduce_scatter x1, waiting for transfers between devices: 76.1 us -> 53.4 us  [per_device(): grads = lax.psum_scatter(stacked, 'tgt', scatter_dimension=0, tiled=True)]
    all_to_all x0 -> x1, blocking collectives: none -> 22.3 us  [per_device(): lax.all_to_all(jnp.stack([err_local] * lax.axis_size('feat')), 'feat', 0, 0)]
where the time goes in v1:
time: 756 us
  waiting for transfers between devices  687 us (91%)
  blocking collectives  31.1 us (4%)
  between operations  17.4 us (2%)
  matrix products  13.7 us (2%)
    unnamed x3, waiting for transfers between devices  634 us
    reduce_scatter x1, waiting for transfers between devices, per_device(): grads = lax.psum_scatter(stacked, 'tgt', scatter_dimension=0, tiled=True)  53.4 us
    all_to_all x1, blocking collectives, per_device(): lax.all_to_all(jnp.stack([err_local] * lax.axis_size('feat')), 'feat', 0, 0)  22.3 us
  transfers between devices with their start and end apart: 2, of which 2 were waited for; matrix products, arithmetic and copies ran while one was open for 0% of the time, Pallas kernels for 0%

profile of v1, /device:TPU:1, one launch (start us, length us, event | category | flops | bytes accessed | tf_op | source)
XLA Modules:
  0.0 756.0 jit_solution(9417950259763940476)
XLA Ops:
  7.2 0.0 copy-start
  7.2 0.0 all-reduce.3.cloned.1.call-start
  7.2 0.8 constant_dynamic-slice_fusion
  8.0 0.7 fusion.64
  9.2 0.0 copy-done
  9.2 1.4 fusion.47
  10.7 8.8 %all-gather = bf16[512,256]{1,0:T(8,128)(2,1)S(1)} all-gather(bf16[128,256]{1,0:T(8,128)(2,1)S(1)} %fusion.47), channel_id=2, replica_groups=mesh['feat'=64,'tgt'=4] {'tgt'}, dimensions={0}, use_global_device_ids=true | all-gather | bytes 327680 | tf_op jit(solution)/shard_map/all_gather | solution.py:13
  21.5 0.0 copy-start.1
  21.5 1.8 convolution_multiply_fusion.3
  23.2 1.6 fusion.2
  24.8 0.0 copy-done.1
  24.9 0.3 fusion.1
  25.2 1.4 fusion
  26.6 0.0 copy-start.4
  26.6 0.0 copy-start.3
  26.6 0.0 all-reduce.3.cloned.1.call-update
  26.6 0.0 reduce-scatter.2.cloned.1.call-start
  26.6 0.6 copy-done.4
  27.2 0.6 dynamic-slice
  28.5 633.8 %all-reduce.3.cloned.1.call-done = f32[128,2304]{1,0:T(8,128)} async-done(((f32[128,2304]{1,0:T(8,128)}), f32[128,2304]{1,0:T(8,128)}) %all-reduce.3.cloned.1.call-update) | async-done | bytes 1179664
  662.3 0.0 copy-done.3
  662.3 0.9 fusion.63
  663.2 0.0 copy-start.2
  663.2 0.3 stack.12
  663.5 22.3 %all_to_all.5 = bf16[64,2,2304]{2,1,0:T(2,128)(2,1)S(1)} all-to-all(bf16[64,2,2304]{2,1,0:T(2,128)(2,1)S(1)} %stack.12), channel_id=1, replica_groups=mesh['feat'=64,'tgt'=4] {'feat'}, dimensions={0} | all-to-all | bytes 1179648 | tf_op jit(solution)/shard_map/all_to_all | solution.py:26
  685.8 0.2 reshape.23
  686.0 0.0 copy-done.2
  686.0 1.8 fusion.26
  687.9 1.8 fusion.32
  689.7 1.8 fusion.38
  691.5 1.8 fusion.44
  693.3 0.8 pad_maximum_fusion
  694.2 0.0 reduce-scatter.2.cloned.1.call-update
  694.2 53.4 %reduce-scatter.2.cloned.1.call-done = f32[1,128,256]{2,1,0:T(8,128)} async-done(((f32[4,128,256]{2,1,0:T(8,128)}), f32[1,128,256]{2,1,0:T(8,128)}) %reduce-scatter.2.cloned.1.call-update) | async-done | bytes 131088 | tf_op jit(solution)/shard_map/reduce_scatter | solution.py:39
  747.6 1.5 convert_element_type.55
Async XLA Ops:
  7.2 2.1 copy-start
  7.2 655.1 %all-reduce.3.cloned.1.call-start = ((), (), s32[]{:S(2)}) async-start(), calls=%async_computation.3 | async-start | bytes 2359296
  21.5 3.4 copy-start.1
  26.6 0.7 copy-start.4
  26.6 635.7 %copy-start.3 = (bf16[1,2,2304]{2,1,0:T(2,128)(2,1)S(1)}, bf16[1,2,2304]{2,1,0:T(2,128)(2,1)}, u32[]{:S(2)}) copy-start(bf16[1,2,2304]{2,1,0:T(2,128)(2,1)} %param.7) | copy-start | bytes 27652
  26.6 721.0 %reduce-scatter.2.cloned.1.call-start = ((), (), s32[]{:S(2)}) async-start(), calls=%async_computation.2 | async-start | bytes 655360 | tf_op jit(solution)/shard_map/reduce_scatter | solution.py:39
  663.2 22.9 %copy-start.2 = (bf16[2,2304]{1,0:T(2,128)(2,1)}, bf16[2,2304]{1,0:T(2,128)(2,1)S(1)}, u32[]{:S(2)}) copy-start(bf16[2,2304]{1,0:T(2,128)(2,1)S(1)} %fusion.63) | copy-start | bytes 27652
Sparse Core Ops, SparseCore 0:
  26.7 635.5 all-reduce.2
  694.3 53.2 reduce-scatter.1
